TPU v7x, 256 devices: a whole 4x4x8 slice. The times are simulated.
256 devices in a mesh: dp: 8 (over y, core), ctx: 32 (over x, z).
Axes of the slice: x: 4, y: 4, z: 8, core: 2. Of those that a mesh axis runs over, the one named last changes fastest.
Arguments:
- queries: bfloat16 [8, 8192, 2560], P('dp', 'ctx'), may hold values from -120 to 120
- global_keys: bfloat16 [8, 8192, 512], P('dp', 'ctx'), may hold values from -5 to 5
- global_values: bfloat16 [8, 8192, 512], P('dp', 'ctx'), may hold values from -6 to 6
- out_grad: bfloat16 [8, 8192, 2560], P('dp', 'ctx'), may hold values from -6 to 6
- query_gain: float32 [2560], replicated, may hold values from 0.5 to 1.5
- doc_start: int32 [8, 64], P('dp', 'ctx'), may hold values from 0 to 63, as said below
Outputs:
- attn_out: bfloat16 [8, 8192, 2560], P('dp', 'ctx')
- query_grad: bfloat16 [8, 8192, 2560], P('dp', 'ctx')
- key_grad: bfloat16 [8, 8192, 512], P('dp', 'ctx')
- value_grad: bfloat16 [8, 8192, 512], P('dp', 'ctx')
- gain_grad: float32 [2560], replicated
Inputs may be any that keep to these rules, and one draw needn't show every extreme that they name: doc_start[g, b] is the first block of block b's document: it is at most b and at least b - 6, never falls along b, and equals b where a document begins; every slab has a document of exactly 7 blocks.
All inputs are finite; a program needn't handle non-finite values.
Results may differ from a plain program's by a relative error of at most 0.017.
The roundings to bfloat16 on the way count: a program that leaves them out, or rounds other values in their place, can miss the bound.
Values may be sent and summed in bfloat16 or wider, within the bound.
No kernel may reach another device: no remote copies, remote signals or barrier semaphores. Data moves between devices by JAX's collectives and lax.ppermute only.
A program may use at most 64 MiB of HBM per device.

v0:
```python
import math
import jax
import jax.numpy as jnp
from jax import lax
from jax.sharding import PartitionSpec as P

HD = 128
BLOCK = 128
REACH = 4


def shifted(value, axis, steps):
    count = lax.axis_size(axis)
    first, last = (max(0, -steps), min(count, count - steps))
    return lax.ppermute(value, axis, [(source, source + steps) for source in range(first, last)])


def head_group(inputs, allowed, factor):
    query_part, key_part, value_part, grad_part = inputs
    scores = (
        jnp.einsum("tgd,wd->gtw", query_part, key_part, preferred_element_type=jnp.float32) * factor
    )
    scores = jnp.where(allowed[None], scores, -jnp.inf)
    row_max = jnp.max(scores, axis=-1, keepdims=True)
    log_total = row_max + jnp.log(jnp.sum(jnp.exp(scores - row_max), axis=-1, keepdims=True))
    weights = jnp.exp(scores - log_total)
    weights_low = weights.astype(jnp.bfloat16)
    result = jnp.einsum(
        "gtw,wd->tgd", weights_low, value_part, preferred_element_type=jnp.float32
    ).astype(jnp.bfloat16)
    inner_sum = jnp.einsum("tgd,tgd->gt", grad_part, result, preferred_element_type=jnp.float32)
    dweights = jnp.einsum("tgd,wd->gtw", grad_part, value_part, preferred_element_type=jnp.float32)
    dscore_low = (weights * (dweights - inner_sum[..., None])).astype(jnp.bfloat16)
    dquery = (
        jnp.einsum("gtw,wd->tgd", dscore_low, key_part, preferred_element_type=jnp.float32) * factor
    )
    dkey = (
        jnp.einsum("gtw,tgd->wd", dscore_low, query_part, preferred_element_type=jnp.float32)
        * factor
    )
    dvalue = jnp.einsum("gtw,tgd->wd", weights_low, grad_part, preferred_element_type=jnp.float32)
    return (result, dquery, dkey, dvalue)


def local(queries, global_keys, global_values, out_grad, query_gain, doc_start):
    row_count = queries.shape[1]
    reach = REACH
    width = reach * row_count
    device = lax.axis_index("ctx")
    query_rows = queries[0]
    key_rows = global_keys[0]
    value_rows = global_values[0]
    grad_rows = out_grad[0]
    kv_count = key_rows.shape[1] // HD
    group_size = query_rows.shape[1] // (kv_count * HD)
    factor = 1.0 / math.sqrt(HD)
    scaled = (query_rows.astype(jnp.float32) * query_gain).astype(jnp.bfloat16)
    key_list = [key_rows]
    value_list = [value_rows]
    for distance in range(1, reach):
        far_keys, far_values = shifted((key_rows, value_rows), "ctx", distance)
        key_list.insert(0, far_keys)
        value_list.insert(0, far_values)
    window_keys = jnp.concatenate(key_list, axis=0)
    window_values = jnp.concatenate(value_list, axis=0)
    first_device = device - (reach - 1)
    query_pos = device * row_count + jnp.arange(row_count, dtype=jnp.int32)
    key_pos = first_device * row_count + jnp.arange(width, dtype=jnp.int32)
    begins = jnp.repeat(doc_start[0], BLOCK) * BLOCK
    allowed = (key_pos[None, :] <= query_pos[:, None]) & (key_pos[None, :] >= begins[:, None])
    query_four = scaled.reshape(row_count, kv_count, group_size, HD).transpose(1, 0, 2, 3)
    grad_four = grad_rows.reshape(row_count, kv_count, group_size, HD).transpose(1, 0, 2, 3)
    key_three = window_keys.reshape(width, kv_count, HD).transpose(1, 0, 2)
    value_three = window_values.reshape(width, kv_count, HD).transpose(1, 0, 2)
    results, dqueries, dkeys, dvalues = lax.map(
        lambda inputs: head_group(inputs, allowed, factor),
        (query_four, key_three, value_three, grad_four),
    )
    attn_out = results.transpose(1, 0, 2, 3).reshape(row_count, -1)
    dscaled = dqueries.transpose(1, 0, 2, 3).reshape(row_count, -1)

    def by_offset(partial_value):
        return partial_value.reshape(kv_count, reach, row_count, HD)[:, ::-1]

    key_offsets = by_offset(dkeys)
    value_offsets = by_offset(dvalues)
    key_total = key_offsets[:, 0]
    value_total = value_offsets[:, 0]
    for distance in range(1, reach):
        got_keys, got_values = shifted(
            (key_offsets[:, distance], value_offsets[:, distance]), "ctx", -distance
        )
        key_total = key_total + got_keys
        value_total = value_total + got_values
    key_grad = key_total.transpose(1, 0, 2).reshape(row_count, -1).astype(jnp.bfloat16)
    value_grad = value_total.transpose(1, 0, 2).reshape(row_count, -1).astype(jnp.bfloat16)
    query_grad = (dscaled * query_gain).astype(jnp.bfloat16)
    gain_term = jnp.sum(dscaled * query_rows.astype(jnp.float32), axis=0)
    gain_grad = lax.psum(gain_term, ("dp", "ctx"))
    return (attn_out[None], query_grad[None], key_grad[None], value_grad[None], gain_grad)


def solution(mesh):
    return jax.shard_map(
        local,
        mesh=mesh,
        in_specs=(
            P("dp", "ctx", None),
            P("dp", "ctx", None),
            P("dp", "ctx", None),
            P("dp", "ctx", None),
            P(),
            P("dp", "ctx"),
        ),
        out_specs=(
            P("dp", "ctx", None),
            P("dp", "ctx", None),
            P("dp", "ctx", None),
            P("dp", "ctx", None),
            P(),
        ),
        check_vma=False,
    )
```

profile of v0, /device:TPU:1, one launch (start us, length us, event | category | flops | bytes accessed | tf_op | source)
XLA Modules:
  0.0 343.3 jit_solution(1276972712751430127)
XLA Ops:
  1.7 5.1 %collective-permute-start.5 = (bf16[256,512]{0,1:T(8,128)(2,1)S(1)}, bf16[256,512]{0,1:T(8,128)(2,1)}, u32[]{:S(2)}, u32[]{:S(2)}) collective-permute-start(bf16[256,512]{0,1:T(8,128)(2,1)S(1)} %bitcast.227), channel_id=1, source_target_pairs={{0,1},{1,2},{2,3},{3,4},{4,5},{5,6},{6,7},{7,8},{8,9},{9,10},{10,1... | collective-permute-start | bytes 786440 | tf_op jit(solution)/shard_map/ppermute | solution.py:15
  6.8 4.9 %collective-permute-start.4 = (bf16[256,512]{0,1:T(8,128)(2,1)S(1)}, bf16[256,512]{0,1:T(8,128)(2,1)}, u32[]{:S(2)}, u32[]{:S(2)}) collective-permute-start(bf16[256,512]{0,1:T(8,128)(2,1)S(1)} %bitcast.228), channel_id=1, source_target_pairs={{0,2},{1,3},{2,4},{3,5},{4,6},{5,7},{6,8},{7,9},{8,10},{9,11},{10,... | collective-permute-start | bytes 786440 | tf_op jit(solution)/shard_map/ppermute | solution.py:15
  11.7 5.7 %collective-permute-start.3 = (bf16[256,512]{0,1:T(8,128)(2,1)S(1)}, bf16[256,512]{0,1:T(8,128)(2,1)}, u32[]{:S(2)}, u32[]{:S(2)}) collective-permute-start(bf16[256,512]{0,1:T(8,128)(2,1)S(1)} %bitcast.229), channel_id=1, source_target_pairs={{0,3},{1,4},{2,5},{3,6},{4,7},{5,8},{6,9},{7,10},{8,11},{9,12},{10... | collective-permute-start | bytes 786440 | tf_op jit(solution)/shard_map/ppermute | solution.py:15
  17.4 2.6 collective-permute-start.2
  20.0 2.3 collective-permute-start.1
  23.1 1.6 copy.41
  24.7 1.7 fusion.35
  26.5 17.9 %collective-permute-done.2 = bf16[256,512]{1,0:T(8,128)(2,1)S(1)} collective-permute-done((bf16[256,512]{1,0:T(8,128)(2,1)}, bf16[256,512]{1,0:T(8,128)(2,1)S(1)}, u32[]{:S(2)}, u32[]{:S(2)}) %collective-permute-start.2) | collective-permute-done | bytes 262176 | tf_op jit(solution)/shard_map/ppermute | solution.py:15
  44.5 9.5 %collective-permute-start = (bf16[256,512]{1,0:T(8,128)(2,1)S(1)}, bf16[256,512]{1,0:T(8,128)(2,1)}, u32[]{:S(2)}, u32[]{:S(2)}) collective-permute-start(bf16[256,512]{1,0:T(8,128)(2,1)S(1)} %bitcast.240), channel_id=1, source_target_pairs={{0,3},{1,4},{2,5},{3,6},{4,7},{5,8},{6,9},{7,10},{8,11},{9,12},{10... | collective-permute-start | bytes 786440 | tf_op jit(solution)/shard_map/ppermute | solution.py:15
  54.1 2.5 copy.42
  58.9 2.2 maximum_bitcast_fusion.1
  63.4 68.0 %while.17 = (s32[]{:T(128)}, bf16[4,256,5,128]{1,3,2,0:T(8,128)(2,1)}, f32[4,256,5,128]{1,3,2,0:T(8,128)}, f32[4,1024,128]{2,1,0:T(8,128)}, f32[4,1024,128]{2,1,...) while((s32[]{:T(128)}, ...), condition=%wide.region_3.4_spmd.clone, body=%wide.region_0.3_spmd.clone.sunk | while | flops 2042689024 | bytes 49229988 | solution.py:75
  65.1 2.0 fusion.71
  68.4 2.2 bitcast_dynamic-update-slice_fusion.2
  70.7 3.1 fusion.75
  73.8 2.6 fusion.72
  76.4 1.7 fusion.74
  78.1 2.3 fusion.73
  82.1 2.0 fusion.71
  85.4 2.2 bitcast_dynamic-update-slice_fusion.2
  87.7 3.1 fusion.75
  90.8 2.6 fusion.72
  93.4 1.6 fusion.74
  95.1 2.3 fusion.73
  99.2 2.0 fusion.71
  102.4 2.2 bitcast_dynamic-update-slice_fusion.2
  104.7 3.1 fusion.75
  107.8 2.6 fusion.72
  110.4 1.6 fusion.74
  112.1 2.3 fusion.73
  116.2 2.0 fusion.71
  119.4 2.2 bitcast_dynamic-update-slice_fusion.2
  121.7 3.1 fusion.75
  124.8 2.6 fusion.72
  127.4 1.6 fusion.74
  129.1 2.3 fusion.73
  131.4 1.7 fusion.46
  134.9 1.4 collective-permute-start.11
  136.4 1.3 collective-permute-start.9
  137.7 1.5 collective-permute-start.10
  143.7 1.3 collective-permute-start.6
  145.0 33.2 %collective-permute-done.11 = f32[4,256,128]{2,0,1:T(4,128)S(1)} collective-permute-done((f32[4,256,128]{2,0,1:T(4,128)S(1)}, f32[4,256,128]{2,0,1:T(4,128)S(1)}, u32[]{:S(2)}, u32[]{:S(2)}) %collective-permute-start.11) | collective-permute-done | bytes 524320 | tf_op jit(solution)/shard_map/ppermute | solution.py:15
  178.2 1.3 collective-permute-start.7
  180.0 2.4 copy.54
  182.4 1.6 copy.55
  184.0 153.9 %psum.7 = f32[2560]{0:T(1024)} all-reduce(f32[2560]{0:T(1024)S(1)} %reduce_sum.21), channel_id=1, replica_groups=mesh['dp'=8,'ctx'=32] {'dp','ctx'}, use_global_device_ids=true, to_apply=%region_5.6 | all-reduce | flops 2560 | bytes 20480 | tf_op jit(solution)/shard_map/psum | solution.py:99
  337.9 1.9 fusion.45
  340.6 1.9 fusion.44
  (98 shorter events, 27.2 us)
Async XLA Ops:
  1.7 57.2 %collective-permute-start.5 = (bf16[256,512]{0,1:T(8,128)(2,1)S(1)}, bf16[256,512]{0,1:T(8,128)(2,1)}, u32[]{:S(2)}, u32[]{:S(2)}) collective-permute-start(bf16[256,512]{0,1:T(8,128)(2,1)S(1)} %bitcast.227), channel_id=1, source_target_pairs={{0,1},{1,2},{2,3},{3,4},{4,5},{5,6},{6,7},{7,8},{8,9},{9,10},{10,1... | collective-permute-start | bytes 786440 | tf_op jit(solution)/shard_map/ppermute | solution.py:15
  6.8 52.1 %collective-permute-start.4 = (bf16[256,512]{0,1:T(8,128)(2,1)S(1)}, bf16[256,512]{0,1:T(8,128)(2,1)}, u32[]{:S(2)}, u32[]{:S(2)}) collective-permute-start(bf16[256,512]{0,1:T(8,128)(2,1)S(1)} %bitcast.228), channel_id=1, source_target_pairs={{0,2},{1,3},{2,4},{3,5},{4,6},{5,7},{6,8},{7,9},{8,10},{9,11},{10,... | collective-permute-start | bytes 786440 | tf_op jit(solution)/shard_map/ppermute | solution.py:15
  11.7 47.2 %collective-permute-start.3 = (bf16[256,512]{0,1:T(8,128)(2,1)S(1)}, bf16[256,512]{0,1:T(8,128)(2,1)}, u32[]{:S(2)}, u32[]{:S(2)}) collective-permute-start(bf16[256,512]{0,1:T(8,128)(2,1)S(1)} %bitcast.229), channel_id=1, source_target_pairs={{0,3},{1,4},{2,5},{3,6},{4,7},{5,8},{6,9},{7,10},{8,11},{9,12},{10... | collective-permute-start | bytes 786440 | tf_op jit(solution)/shard_map/ppermute | solution.py:15
  17.4 27.1 %collective-permute-start.2 = (bf16[256,512]{1,0:T(8,128)(2,1)}, bf16[256,512]{1,0:T(8,128)(2,1)S(1)}, u32[]{:S(2)}, u32[]{:S(2)}) collective-permute-start(bf16[256,512]{1,0:T(8,128)(2,1)} %bitcast.238), channel_id=1, source_target_pairs={{0,1},{1,2},{2,3},{3,4},{4,5},{5,6},{6,7},{7,8},{8,9},{9,10},{10,1... | collective-permute-start | bytes 786440 | tf_op jit(solution)/shard_map/ppermute | solution.py:15
  20.0 37.7 %collective-permute-start.1 = (bf16[256,512]{1,0:T(8,128)(2,1)}, bf16[256,512]{1,0:T(8,128)(2,1)}, u32[]{:S(2)}, u32[]{:S(2)}) collective-permute-start(bf16[256,512]{1,0:T(8,128)(2,1)} %bitcast.239), channel_id=1, source_target_pairs={{0,2},{1,3},{2,4},{3,5},{4,6},{5,7},{6,8},{7,9},{8,10},{9,11},{10,... | collective-permute-start | bytes 786440 | tf_op jit(solution)/shard_map/ppermute | solution.py:15
  24.7 31.9 %copy-start = (f32[1,256,2560]{1,2,0:T(8,128)}, f32[1,256,2560]{1,2,0:T(8,128)S(1)}, u32[]{:S(2)}) copy-start(f32[1,256,2560]{1,2,0:T(8,128)S(1)} %copy.41) | copy-start | bytes 7864324
  24.7 1.8 copy-start.10
  24.7 19.7 %copy-start.7 = (bf16[1,256,512]{2,1,0:T(8,128)(2,1)S(1)}, bf16[1,256,512]{2,1,0:T(8,128)(2,1)}, u32[]{:S(2)}) copy-start(bf16[1,256,512]{2,1,0:T(8,128)(2,1)} %param.10) | copy-start | bytes 786436
  44.5 9.5 %copy-start.8 = (bf16[256,512]{1,0:T(8,128)(2,1)}, bf16[256,512]{1,0:T(8,128)(2,1)S(1)}, u32[]{:S(2)}) copy-start(bf16[256,512]{1,0:T(8,128)(2,1)S(1)} %collective-permute-done.2) | copy-start | bytes 786436
  44.5 16.7 %collective-permute-start = (bf16[256,512]{1,0:T(8,128)(2,1)S(1)}, bf16[256,512]{1,0:T(8,128)(2,1)}, u32[]{:S(2)}, u32[]{:S(2)}) collective-permute-start(bf16[256,512]{1,0:T(8,128)(2,1)S(1)} %bitcast.240), channel_id=1, source_target_pairs={{0,3},{1,4},{2,5},{3,6},{4,7},{5,8},{6,9},{7,10},{8,11},{9,12},{10... | collective-permute-start | bytes 786440 | tf_op jit(solution)/shard_map/ppermute | solution.py:15
  57.7 5.7 %copy-start.2 = (bf16[4,256,5,128]{1,3,2,0:T(8,128)(2,1)S(1)}, bf16[4,256,5,128]{1,3,2,0:T(8,128)(2,1)}, u32[]{:S(2)}) copy-start(bf16[4,256,5,128]{1,3,2,0:T(8,128)(2,1)} %fusion.35) | copy-start | bytes 3932164
  67.1 1.2 copy-start.5
  84.1 1.2 copy-start.5
  101.1 1.2 copy-start.5
  118.2 1.2 copy-start.5
  133.1 6.1 %copy-start.3 = (f32[4,256,5,128]{1,3,2,0:T(8,128)S(1)}, f32[4,256,5,128]{1,3,2,0:T(8,128)}, u32[]{:S(2)}) copy-start(f32[4,256,5,128]{1,3,2,0:T(8,128)} %get-tuple-element.61) | copy-start | bytes 7864324
  133.1 6.1 %copy-start.9 = (f32[2560]{0:T(1024)S(1)}, f32[2560]{0:T(1024)}, u32[]{:S(2)}) copy-start(f32[2560]{0:T(1024)} %param.12) | copy-start | bytes 30724
  134.6 5.0 %copy-start.4 = (f32[4,1024,128]{2,1,0:T(8,128)S(1)}, f32[4,1024,128]{2,1,0:T(8,128)}, u32[]{:S(2)}) copy-start(f32[4,1024,128]{2,1,0:T(8,128)} %get-tuple-element.62) | copy-start | bytes 6291460
  134.9 43.2 %collective-permute-start.11 = (f32[4,256,128]{2,0,1:T(4,128)S(1)}, f32[4,256,128]{2,0,1:T(4,128)S(1)}, u32[]{:S(2)}, u32[]{:S(2)}) collective-permute-start(f32[4,256,128]{2,0,1:T(4,128)S(1)} %bitcast.237), channel_id=1, source_target_pairs={{3,0},{4,1},{5,2},{6,3},{7,4},{8,5},{9,6},{10,7},{11,8},{12,9},{13... | collective-permute-start | bytes 1572872 | tf_op jit(solution)/shard_map/ppermute | solution.py:15
  136.4 201.5 %collective-permute-start.9 = (f32[4,256,128]{2,0,1:T(4,128)}, f32[4,256,128]{2,0,1:T(4,128)}, u32[]{:S(2)}, u32[]{:S(2)}) collective-permute-start(f32[4,256,128]{2,0,1:T(4,128)} %bitcast.170), channel_id=1, source_target_pairs={{1,0},{2,1},{3,2},{4,3},{5,4},{6,5},{7,6},{8,7},{9,8},{10,9},{11,1... | collective-permute-start | bytes 1572872 | tf_op jit(solution)/shard_map/ppermute | solution.py:15
  137.7 200.2 %collective-permute-start.10 = (f32[4,256,128]{2,0,1:T(4,128)S(1)}, f32[4,256,128]{2,0,1:T(4,128)}, u32[]{:S(2)}, u32[]{:S(2)}) collective-permute-start(f32[4,256,128]{2,0,1:T(4,128)S(1)} %bitcast.235), channel_id=1, source_target_pairs={{2,0},{3,1},{4,2},{5,3},{6,4},{7,5},{8,6},{9,7},{10,8},{11,9},{12,... | collective-permute-start | bytes 1572872 | tf_op jit(solution)/shard_map/ppermute | solution.py:15
  139.8 39.7 %copy-start.1 = (f32[1,256,2560]{1,2,0:T(8,128)S(1)}, f32[1,256,2560]{1,2,0:T(8,128)}, u32[]{:S(2)}) copy-start(f32[1,256,2560]{1,2,0:T(8,128)} %copy-done) | copy-start | bytes 7864324
  142.4 198.2 %collective-permute-start.8 = (f32[4,256,128]{2,0,1:T(4,128)}, f32[4,256,128]{2,0,1:T(4,128)}, u32[]{:S(2)}, u32[]{:S(2)}) collective-permute-start(f32[4,256,128]{2,0,1:T(4,128)} %bitcast.171), channel_id=1, source_target_pairs={{3,0},{4,1},{5,2},{6,3},{7,4},{8,5},{9,6},{10,7},{11,8},{12,9},{13... | collective-permute-start | bytes 1572872 | tf_op jit(solution)/shard_map/ppermute | solution.py:15
  143.7 196.9 %collective-permute-start.6 = (f32[4,256,128]{2,0,1:T(4,128)}, f32[4,256,128]{2,0,1:T(4,128)}, u32[]{:S(2)}, u32[]{:S(2)}) collective-permute-start(f32[4,256,128]{2,0,1:T(4,128)} %bitcast.173), channel_id=1, source_target_pairs={{1,0},{2,1},{3,2},{4,3},{5,4},{6,5},{7,6},{8,7},{9,8},{10,9},{11,1... | collective-permute-start | bytes 1572872 | tf_op jit(solution)/shard_map/ppermute | solution.py:15
  178.2 1.3 copy-start.6
  178.2 162.4 %collective-permute-start.7 = (f32[4,256,128]{2,0,1:T(4,128)S(1)}, f32[4,256,128]{2,0,1:T(4,128)}, u32[]{:S(2)}, u32[]{:S(2)}) collective-permute-start(f32[4,256,128]{2,0,1:T(4,128)S(1)} %bitcast.236), channel_id=1, source_target_pairs={{2,0},{3,1},{4,2},{5,3},{6,4},{7,5},{8,6},{9,7},{10,8},{11,9},{12,... | collective-permute-start | bytes 1572872 | tf_op jit(solution)/shard_map/ppermute | solution.py:15
where the time goes:
time: 345 us; the launch traced here: 343 us
  blocking collectives  154 us (45%)
  matrix products  55.5 us (16%)
  waiting for transfers between devices  51.1 us (15%)
  starting transfers between devices  38.2 us (11%)
  local copies, waits for them, and re-layouts  27.5 us (8%)
  other arithmetic  15.8 us (5%)
    psum x1, blocking collectives, local(): gain_grad = lax.psum(gain_term, ('dp', 'ctx'))  154 us
    ppermute x12, waiting for transfers between devices, shifted(): lax.ppermute(value, axis, [(source, source + steps) for source in range(f...  51.1 us
    ppermute x12, starting transfers between devices, shifted(): lax.ppermute(value, axis, [(source, source + steps) for source in range(f...  38.2 us
    dot_general x4, matrix products, head_group(): jnp.einsum('gtw,tgd->wd', weights_low, grad_part, preferred_element_type=...  12.5 us
    unnamed x31, local copies, waits for them, and re-layouts  12.2 us
    dot_general x4, matrix products, head_group(): jnp.einsum('tgd,wd->gtw', grad_part, value_part, preferred_element_type=j...  10.4 us
    dot_general x4, matrix products, head_group(): jnp.einsum('gtw,wd->tgd', dscore_low, key_part, preferred_element_type=jn...  9.25 us
    dot_general x4, matrix products, head_group(): jnp.einsum('gtw,wd->tgd', weights_low, value_part, preferred_element_type...  8.8 us
  transfers between devices with their start and end apart: 12, of which 2 were waited for; matrix products, arithmetic and copies ran while one was open for 6% of the time, Pallas kernels for 0%

commit v1 on v0

--- a/solution.py
+++ b/solution.py
@@ -96,7 +96,7 @@
     value_grad = value_total.transpose(1, 0, 2).reshape(row_count, -1).astype(jnp.bfloat16)
     query_grad = (dscaled * query_gain).astype(jnp.bfloat16)
     gain_term = jnp.sum(dscaled * query_rows.astype(jnp.float32), axis=0)
-    gain_grad = lax.psum(gain_term, ("dp", "ctx"))
+    gain_grad = lax.psum(lax.psum(gain_term, "ctx"), "dp")
     return (attn_out[None], query_grad[None], key_grad[None], value_grad[None], gain_grad)
 
 

time: 345 us -> 450 us (1.30)
  blocking collectives: 154 us -> 259 us
    psum x1 -> x2, blocking collectives: 154 us -> 259 us  [local(): gain_grad = lax.psum(lax.psum(gain_term, 'ctx'), 'dp')]
  transfers between devices with their start and end apart: 12 -> 12, of which waited for: 2 -> 2; matrix products, arithmetic and copies ran while one was open for 6% -> 5% of each run, Pallas kernels for 0% -> 0%
where the time goes in v1:
time: 450 us; the launch traced here: 448 us
  blocking collectives  259 us (58%)
  matrix products  55.5 us (12%)
  waiting for transfers between devices  51.1 us (11%)
  starting transfers between devices  38.2 us (8%)
  local copies, waits for them, and re-layouts  27.5 us (6%)
  other arithmetic  15.9 us (4%)
    psum x2, blocking collectives, local(): gain_grad = lax.psum(lax.psum(gain_term, 'ctx'), 'dp')  259 us
    ppermute x12, waiting for transfers between devices, shifted(): lax.ppermute(value, axis, [(source, source + steps) for source in range(f...  51.1 us
    ppermute x12, starting transfers between devices, shifted(): lax.ppermute(value, axis, [(source, source + steps) for source in range(f...  38.2 us
    dot_general x4, matrix products, head_group(): jnp.einsum('gtw,tgd->wd', weights_low, grad_part, preferred_element_type=...  12.6 us
    unnamed x31, local copies, waits for them, and re-layouts  12.2 us
    dot_general x4, matrix products, head_group(): jnp.einsum('tgd,wd->gtw', grad_part, value_part, preferred_element_type=j...  10.4 us
    dot_general x4, matrix products, head_group(): jnp.einsum('gtw,wd->tgd', dscore_low, key_part, preferred_element_type=jn...  9.23 us
  transfers between devices with their start and end apart: 12, of which 2 were waited for; matrix products, arithmetic and copies ran while one was open for 5% of the time, Pallas kernels for 0%

profile of v1, /device:TPU:1, one launch (start us, length us, event | category | flops | bytes accessed | tf_op | source)
XLA Modules:
  0.0 448.1 jit_solution(16250482573742724201)
XLA Ops:
  1.7 5.1 %collective-permute-start.5 = (bf16[256,512]{0,1:T(8,128)(2,1)S(1)}, bf16[256,512]{0,1:T(8,128)(2,1)}, u32[]{:S(2)}, u32[]{:S(2)}) collective-permute-start(bf16[256,512]{0,1:T(8,128)(2,1)S(1)} %bitcast.227), channel_id=1, source_target_pairs={{0,1},{1,2},{2,3},{3,4},{4,5},{5,6},{6,7},{7,8},{8,9},{9,10},{10,1... | collective-permute-start | bytes 786440 | tf_op jit(solution)/shard_map/ppermute | solution.py:15
  6.8 4.9 %collective-permute-start.4 = (bf16[256,512]{0,1:T(8,128)(2,1)S(1)}, bf16[256,512]{0,1:T(8,128)(2,1)}, u32[]{:S(2)}, u32[]{:S(2)}) collective-permute-start(bf16[256,512]{0,1:T(8,128)(2,1)S(1)} %bitcast.228), channel_id=1, source_target_pairs={{0,2},{1,3},{2,4},{3,5},{4,6},{5,7},{6,8},{7,9},{8,10},{9,11},{10,... | collective-permute-start | bytes 786440 | tf_op jit(solution)/shard_map/ppermute | solution.py:15
  11.7 5.7 %collective-permute-start.3 = (bf16[256,512]{0,1:T(8,128)(2,1)S(1)}, bf16[256,512]{0,1:T(8,128)(2,1)}, u32[]{:S(2)}, u32[]{:S(2)}) collective-permute-start(bf16[256,512]{0,1:T(8,128)(2,1)S(1)} %bitcast.229), channel_id=1, source_target_pairs={{0,3},{1,4},{2,5},{3,6},{4,7},{5,8},{6,9},{7,10},{8,11},{9,12},{10... | collective-permute-start | bytes 786440 | tf_op jit(solution)/shard_map/ppermute | solution.py:15
  17.4 2.6 collective-permute-start.2
  20.0 2.3 collective-permute-start.1
  23.1 1.6 copy.41
  24.7 1.7 fusion.35
  26.5 17.9 %collective-permute-done.2 = bf16[256,512]{1,0:T(8,128)(2,1)S(1)} collective-permute-done((bf16[256,512]{1,0:T(8,128)(2,1)}, bf16[256,512]{1,0:T(8,128)(2,1)S(1)}, u32[]{:S(2)}, u32[]{:S(2)}) %collective-permute-start.2) | collective-permute-done | bytes 262176 | tf_op jit(solution)/shard_map/ppermute | solution.py:15
  44.5 9.5 %collective-permute-start = (bf16[256,512]{1,0:T(8,128)(2,1)S(1)}, bf16[256,512]{1,0:T(8,128)(2,1)}, u32[]{:S(2)}, u32[]{:S(2)}) collective-permute-start(bf16[256,512]{1,0:T(8,128)(2,1)S(1)} %bitcast.240), channel_id=1, source_target_pairs={{0,3},{1,4},{2,5},{3,6},{4,7},{5,8},{6,9},{7,10},{8,11},{9,12},{10... | collective-permute-start | bytes 786440 | tf_op jit(solution)/shard_map/ppermute | solution.py:15
  54.1 2.5 copy.42
  58.9 2.2 maximum_bitcast_fusion.1
  63.4 68.1 %while.17 = (s32[]{:T(128)}, bf16[4,256,5,128]{1,3,2,0:T(8,128)(2,1)}, f32[4,256,5,128]{1,3,2,0:T(8,128)}, f32[4,1024,128]{2,1,0:T(8,128)}, f32[4,1024,128]{2,1,...) while((s32[]{:T(128)}, ...), condition=%wide.region_3.4_spmd.clone, body=%wide.region_0.3_spmd.clone.sunk | while | flops 2042689024 | bytes 49229988 | solution.py:75
  65.2 2.0 fusion.71
  68.4 2.2 bitcast_dynamic-update-slice_fusion.2
  70.7 3.1 fusion.75
  73.8 2.6 fusion.72
  76.4 1.7 fusion.74
  78.1 2.3 fusion.73
  82.2 2.0 fusion.71
  85.4 2.2 bitcast_dynamic-update-slice_fusion.2
  87.7 3.2 fusion.75
  90.8 2.6 fusion.72
  93.4 1.6 fusion.74
  95.1 2.3 fusion.73
  99.2 2.0 fusion.71
  102.4 2.2 bitcast_dynamic-update-slice_fusion.2
  104.7 3.1 fusion.75
  107.9 2.6 fusion.72
  110.5 1.7 fusion.74
  112.1 2.3 fusion.73
  116.2 2.0 fusion.71
  119.4 2.2 bitcast_dynamic-update-slice_fusion.2
  121.7 3.2 fusion.75
  124.9 2.6 fusion.72
  127.5 1.7 fusion.74
  129.2 2.3 fusion.73
  131.5 1.7 fusion.46
  135.1 1.4 collective-permute-start.11
  136.5 1.3 collective-permute-start.9
  137.8 1.5 collective-permute-start.10
  143.8 1.3 collective-permute-start.6
  145.1 33.2 %collective-permute-done.11 = f32[4,256,128]{2,0,1:T(4,128)S(1)} collective-permute-done((f32[4,256,128]{2,0,1:T(4,128)S(1)}, f32[4,256,128]{2,0,1:T(4,128)S(1)}, u32[]{:S(2)}, u32[]{:S(2)}) %collective-permute-start.11) | collective-permute-done | bytes 524320 | tf_op jit(solution)/shard_map/ppermute | solution.py:15
  180.1 2.4 copy.54
  182.5 1.6 copy.55
  184.1 210.0 %psum.14 = f32[2560]{0:T(1024)S(1)} all-reduce(f32[2560]{0:T(1024)S(1)} %reduce_sum.21), channel_id=1, replica_groups=mesh['dp'=8,'ctx'=32] {'ctx'}, use_global_device_ids=true, to_apply=%region_5.6 | all-reduce | flops 2560 | bytes 20480 | tf_op jit(solution)/shard_map/psum | solution.py:99
  394.1 48.6 %psum.15 = f32[2560]{0:T(1024)} all-reduce(f32[2560]{0:T(1024)S(1)} %psum.14), channel_id=1, replica_groups=mesh['dp'=8,'ctx'=32] {'dp'}, use_global_device_ids=true, to_apply=%region_6.7 | all-reduce | flops 2560 | bytes 20480 | tf_op jit(solution)/shard_map/psum | solution.py:99
  442.7 1.9 fusion.45
  445.4 1.9 fusion.44
  (99 shorter events, 28.5 us)
Async XLA Ops:
  1.7 57.1 %collective-permute-start.5 = (bf16[256,512]{0,1:T(8,128)(2,1)S(1)}, bf16[256,512]{0,1:T(8,128)(2,1)}, u32[]{:S(2)}, u32[]{:S(2)}) collective-permute-start(bf16[256,512]{0,1:T(8,128)(2,1)S(1)} %bitcast.227), channel_id=1, source_target_pairs={{0,1},{1,2},{2,3},{3,4},{4,5},{5,6},{6,7},{7,8},{8,9},{9,10},{10,1... | collective-permute-start | bytes 786440 | tf_op jit(solution)/shard_map/ppermute | solution.py:15
  6.8 52.1 %collective-permute-start.4 = (bf16[256,512]{0,1:T(8,128)(2,1)S(1)}, bf16[256,512]{0,1:T(8,128)(2,1)}, u32[]{:S(2)}, u32[]{:S(2)}) collective-permute-start(bf16[256,512]{0,1:T(8,128)(2,1)S(1)} %bitcast.228), channel_id=1, source_target_pairs={{0,2},{1,3},{2,4},{3,5},{4,6},{5,7},{6,8},{7,9},{8,10},{9,11},{10,... | collective-permute-start | bytes 786440 | tf_op jit(solution)/shard_map/ppermute | solution.py:15
  11.7 47.2 %collective-permute-start.3 = (bf16[256,512]{0,1:T(8,128)(2,1)S(1)}, bf16[256,512]{0,1:T(8,128)(2,1)}, u32[]{:S(2)}, u32[]{:S(2)}) collective-permute-start(bf16[256,512]{0,1:T(8,128)(2,1)S(1)} %bitcast.229), channel_id=1, source_target_pairs={{0,3},{1,4},{2,5},{3,6},{4,7},{5,8},{6,9},{7,10},{8,11},{9,12},{10... | collective-permute-start | bytes 786440 | tf_op jit(solution)/shard_map/ppermute | solution.py:15
  17.4 27.1 %collective-permute-start.2 = (bf16[256,512]{1,0:T(8,128)(2,1)}, bf16[256,512]{1,0:T(8,128)(2,1)S(1)}, u32[]{:S(2)}, u32[]{:S(2)}) collective-permute-start(bf16[256,512]{1,0:T(8,128)(2,1)} %bitcast.238), channel_id=1, source_target_pairs={{0,1},{1,2},{2,3},{3,4},{4,5},{5,6},{6,7},{7,8},{8,9},{9,10},{10,1... | collective-permute-start | bytes 786440 | tf_op jit(solution)/shard_map/ppermute | solution.py:15
  20.0 37.6 %collective-permute-start.1 = (bf16[256,512]{1,0:T(8,128)(2,1)}, bf16[256,512]{1,0:T(8,128)(2,1)}, u32[]{:S(2)}, u32[]{:S(2)}) collective-permute-start(bf16[256,512]{1,0:T(8,128)(2,1)} %bitcast.239), channel_id=1, source_target_pairs={{0,2},{1,3},{2,4},{3,5},{4,6},{5,7},{6,8},{7,9},{8,10},{9,11},{10,... | collective-permute-start | bytes 786440 | tf_op jit(solution)/shard_map/ppermute | solution.py:15
  24.7 31.9 %copy-start = (f32[1,256,2560]{1,2,0:T(8,128)}, f32[1,256,2560]{1,2,0:T(8,128)S(1)}, u32[]{:S(2)}) copy-start(f32[1,256,2560]{1,2,0:T(8,128)S(1)} %copy.41) | copy-start | bytes 7864324
  24.7 1.8 copy-start.10
  24.7 19.7 %copy-start.7 = (bf16[1,256,512]{2,1,0:T(8,128)(2,1)S(1)}, bf16[1,256,512]{2,1,0:T(8,128)(2,1)}, u32[]{:S(2)}) copy-start(bf16[1,256,512]{2,1,0:T(8,128)(2,1)} %param.10) | copy-start | bytes 786436
  44.5 9.5 %copy-start.8 = (bf16[256,512]{1,0:T(8,128)(2,1)}, bf16[256,512]{1,0:T(8,128)(2,1)S(1)}, u32[]{:S(2)}) copy-start(bf16[256,512]{1,0:T(8,128)(2,1)S(1)} %collective-permute-done.2) | copy-start | bytes 786436
  44.5 16.7 %collective-permute-start = (bf16[256,512]{1,0:T(8,128)(2,1)S(1)}, bf16[256,512]{1,0:T(8,128)(2,1)}, u32[]{:S(2)}, u32[]{:S(2)}) collective-permute-start(bf16[256,512]{1,0:T(8,128)(2,1)S(1)} %bitcast.240), channel_id=1, source_target_pairs={{0,3},{1,4},{2,5},{3,6},{4,7},{5,8},{6,9},{7,10},{8,11},{9,12},{10... | collective-permute-start | bytes 786440 | tf_op jit(solution)/shard_map/ppermute | solution.py:15
  57.7 5.7 %copy-start.2 = (bf16[4,256,5,128]{1,3,2,0:T(8,128)(2,1)S(1)}, bf16[4,256,5,128]{1,3,2,0:T(8,128)(2,1)}, u32[]{:S(2)}) copy-start(bf16[4,256,5,128]{1,3,2,0:T(8,128)(2,1)} %fusion.35) | copy-start | bytes 3932164
  67.1 1.2 copy-start.5
  84.1 1.2 copy-start.5
  101.2 1.2 copy-start.5
  118.2 1.2 copy-start.5
  133.1 6.1 %copy-start.3 = (f32[4,256,5,128]{1,3,2,0:T(8,128)S(1)}, f32[4,256,5,128]{1,3,2,0:T(8,128)}, u32[]{:S(2)}) copy-start(f32[4,256,5,128]{1,3,2,0:T(8,128)} %get-tuple-element.61) | copy-start | bytes 7864324
  133.2 6.1 %copy-start.9 = (f32[2560]{0:T(1024)S(1)}, f32[2560]{0:T(1024)}, u32[]{:S(2)}) copy-start(f32[2560]{0:T(1024)} %param.12) | copy-start | bytes 30724
  134.7 5.0 %copy-start.4 = (f32[4,1024,128]{2,1,0:T(8,128)S(1)}, f32[4,1024,128]{2,1,0:T(8,128)}, u32[]{:S(2)}) copy-start(f32[4,1024,128]{2,1,0:T(8,128)} %get-tuple-element.62) | copy-start | bytes 6291460
  135.1 43.2 %collective-permute-start.11 = (f32[4,256,128]{2,0,1:T(4,128)S(1)}, f32[4,256,128]{2,0,1:T(4,128)S(1)}, u32[]{:S(2)}, u32[]{:S(2)}) collective-permute-start(f32[4,256,128]{2,0,1:T(4,128)S(1)} %bitcast.237), channel_id=1, source_target_pairs={{3,0},{4,1},{5,2},{6,3},{7,4},{8,5},{9,6},{10,7},{11,8},{12,9},{13... | collective-permute-start | bytes 1572872 | tf_op jit(solution)/shard_map/ppermute | solution.py:15
  136.5 306.2 %collective-permute-start.9 = (f32[4,256,128]{2,0,1:T(4,128)}, f32[4,256,128]{2,0,1:T(4,128)}, u32[]{:S(2)}, u32[]{:S(2)}) collective-permute-start(f32[4,256,128]{2,0,1:T(4,128)} %bitcast.170), channel_id=1, source_target_pairs={{1,0},{2,1},{3,2},{4,3},{5,4},{6,5},{7,6},{8,7},{9,8},{10,9},{11,1... | collective-permute-start | bytes 1572872 | tf_op jit(solution)/shard_map/ppermute | solution.py:15
  137.8 304.9 %collective-permute-start.10 = (f32[4,256,128]{2,0,1:T(4,128)S(1)}, f32[4,256,128]{2,0,1:T(4,128)}, u32[]{:S(2)}, u32[]{:S(2)}) collective-permute-start(f32[4,256,128]{2,0,1:T(4,128)S(1)} %bitcast.235), channel_id=1, source_target_pairs={{2,0},{3,1},{4,2},{5,3},{6,4},{7,5},{8,6},{9,7},{10,8},{11,9},{12,... | collective-permute-start | bytes 1572872 | tf_op jit(solution)/shard_map/ppermute | solution.py:15
  139.9 39.7 %copy-start.1 = (f32[1,256,2560]{1,2,0:T(8,128)S(1)}, f32[1,256,2560]{1,2,0:T(8,128)}, u32[]{:S(2)}) copy-start(f32[1,256,2560]{1,2,0:T(8,128)} %copy-done) | copy-start | bytes 7864324
  142.5 302.9 %collective-permute-start.8 = (f32[4,256,128]{2,0,1:T(4,128)}, f32[4,256,128]{2,0,1:T(4,128)}, u32[]{:S(2)}, u32[]{:S(2)}) collective-permute-start(f32[4,256,128]{2,0,1:T(4,128)} %bitcast.171), channel_id=1, source_target_pairs={{3,0},{4,1},{5,2},{6,3},{7,4},{8,5},{9,6},{10,7},{11,8},{12,9},{13... | collective-permute-start | bytes 1572872 | tf_op jit(solution)/shard_map/ppermute | solution.py:15
  143.8 301.6 %collective-permute-start.6 = (f32[4,256,128]{2,0,1:T(4,128)}, f32[4,256,128]{2,0,1:T(4,128)}, u32[]{:S(2)}, u32[]{:S(2)}) collective-permute-start(f32[4,256,128]{2,0,1:T(4,128)} %bitcast.173), channel_id=1, source_target_pairs={{1,0},{2,1},{3,2},{4,3},{5,4},{6,5},{7,6},{8,7},{9,8},{10,9},{11,1... | collective-permute-start | bytes 1572872 | tf_op jit(solution)/shard_map/ppermute | solution.py:15
  178.3 1.3 copy-start.6
  178.3 267.1 %collective-permute-start.7 = (f32[4,256,128]{2,0,1:T(4,128)S(1)}, f32[4,256,128]{2,0,1:T(4,128)}, u32[]{:S(2)}, u32[]{:S(2)}) collective-permute-start(f32[4,256,128]{2,0,1:T(4,128)S(1)} %bitcast.236), channel_id=1, source_target_pairs={{2,0},{3,1},{4,2},{5,3},{6,4},{7,5},{8,6},{9,7},{10,8},{11,9},{12,... | collective-permute-start | bytes 1572872 | tf_op jit(solution)/shard_map/ppermute | solution.py:15
